TPU v7x, 32 devices: a whole 2x2x4 slice. The times are simulated.
32 devices in a mesh: expert: 16 (over z, y, x), tok: 2 (over core).
Axes of the slice: x: 2, y: 2, z: 4, core: 2. Of those that a mesh axis runs over, the one named last changes fastest.
Arguments:
- tokens: bfloat16 [2048, 3584], P(('expert', 'tok')), may hold values from -6 to 6
- routes: int32 [2048, 8], P(('expert', 'tok')), may hold values from 0 to 15, all different within a row; in each aligned block of 64 rows (0 to 63, 64 to 127, ...) at most 36 rows name the same one
- gates: float32 [2048, 8], P(('expert', 'tok')), may hold values from 0.05 to 1
- upstream: bfloat16 [2048, 3584], P(('expert', 'tok')), may hold values from -6 to 6
- w_up: bfloat16 [16, 3584, 1024], P('expert', None, 'tok'), may hold values from -0.09375 to 0.09375
- w_down: bfloat16 [16, 1024, 3584], P('expert', 'tok'), may hold values from -0.1875 to 0.1875
Outputs:
- mixed: bfloat16 [2048, 3584], P(('expert', 'tok'))
- d_tokens: bfloat16 [2048, 3584], P(('expert', 'tok'))
- d_gates: float32 [2048, 8], P(('expert', 'tok'))
- grad_up: bfloat16 [16, 3584, 1024], P('expert', None, 'tok')
- grad_down: bfloat16 [16, 1024, 3584], P('expert', 'tok')
Inputs may be any that keep to these rules, and one draw needn't show every extreme that they name: `routes`: each token names 8 different experts. At most 36 of the 64 tokens of one device name the same expert, and in every draw the tokens of some device name some expert exactly 36 times.
All inputs are finite; a program needn't handle non-finite values.
Results may differ from a plain program's by a relative error of at most 0.0065.
Values may be sent and summed in bfloat16 or wider, within the bound.
A program may use at most 192 MiB of HBM per device.

v0:
```python
import jax
import jax.numpy as jnp
from jax import lax
from jax.sharding import PartitionSpec as P

GELU_C = 0.7978845608028654
GELU_A = 0.044715


def gelu_value(hidden):
    inner_arg = GELU_C * (hidden + GELU_A * hidden * hidden * hidden)
    return 0.5 * hidden * (1.0 + jnp.tanh(inner_arg))


def gelu_slope(hidden):
    tangent = jnp.tanh(GELU_C * (hidden + GELU_A * hidden * hidden * hidden))
    return 0.5 * (1.0 + tangent) + 0.5 * hidden * (1.0 - tangent * tangent) * GELU_C * (
        1.0 + 3.0 * GELU_A * hidden * hidden
    )


def expert_rows(rows_x, rows_grad, up_local, down_local):
    hidden = jnp.dot(rows_x, up_local, preferred_element_type=jnp.float32)
    active = gelu_value(hidden).astype(jnp.bfloat16)
    out_part = jnp.dot(active, down_local, preferred_element_type=jnp.float32)
    d_active = lax.dot_general(
        rows_grad, down_local, (((1,), (1,)), ((), ())), preferred_element_type=jnp.float32
    )
    d_hidden = (d_active * gelu_slope(hidden)).astype(jnp.bfloat16)
    dx_part = lax.dot_general(
        d_hidden, up_local, (((1,), (1,)), ((), ())), preferred_element_type=jnp.float32
    )
    grad_down = lax.dot_general(
        active, rows_grad, (((0,), (0,)), ((), ())), preferred_element_type=jnp.float32
    )
    grad_up = lax.dot_general(
        rows_x, d_hidden, (((0,), (0,)), ((), ())), preferred_element_type=jnp.float32
    )
    return (out_part, dx_part, grad_up, grad_down)


def routed_shards(tokens, routes, gates, upstream, w_up, w_down):
    tok_rows, feature_width = tokens.shape
    top_count = routes.shape[1]
    owners = lax.axis_size("expert")
    pair_count = lax.axis_size("tok")
    capacity = tok_rows * top_count // owners + max(1, tok_rows * top_count // (8 * owners))
    assigned = routes.reshape(-1)
    labels = jnp.arange(owners, dtype=jnp.int32)
    onehot = (assigned[:, None] == labels[None, :]).astype(jnp.int32)
    earlier = jnp.cumsum(onehot, axis=0) - onehot
    slot_rank = jnp.sum(earlier * onehot, axis=1)
    slot_of = assigned * capacity + slot_rank
    slot_ids = jnp.arange(owners * capacity, dtype=jnp.int32)
    matches = (slot_of[None, :] == slot_ids[:, None]).astype(jnp.int32)
    filled = jnp.sum(matches, axis=1) > 0
    source = jnp.sum(matches * jnp.arange(assigned.shape[0], dtype=jnp.int32)[None, :], axis=1)
    token_ids = source // top_count
    send_x = jnp.where(filled[:, None], tokens[token_ids], jnp.zeros((), jnp.bfloat16))
    gate_rows = jnp.where(filled, gates.reshape(-1)[source], jnp.zeros((), jnp.float32))
    send_grad = (gate_rows[:, None] * upstream[token_ids].astype(jnp.float32)).astype(jnp.bfloat16)
    send_x = send_x.reshape(owners, capacity, feature_width)
    send_grad = send_grad.reshape(owners, capacity, feature_width)
    recv_x, recv_grad = (
        lax.all_to_all(send_x, "expert", split_axis=0, concat_axis=0, tiled=True),
        lax.all_to_all(send_grad, "expert", split_axis=0, concat_axis=0, tiled=True),
    )
    both_x, both_grad = (
        lax.all_gather(recv_x[None], "tok", axis=0, tiled=True),
        lax.all_gather(recv_grad[None], "tok", axis=0, tiled=True),
    )
    rows_x = both_x.reshape(-1, feature_width)
    rows_grad = both_grad.reshape(-1, feature_width)
    out_part, dx_part, grad_up, grad_down = expert_rows(rows_x, rows_grad, w_up[0], w_down[0])
    shaped_out = out_part.reshape(pair_count, owners, capacity, feature_width)
    shaped_dx = dx_part.reshape(pair_count, owners, capacity, feature_width)
    summed_out, summed_dx = (
        lax.psum_scatter(shaped_out, "tok", scatter_dimension=0, tiled=True),
        lax.psum_scatter(shaped_dx, "tok", scatter_dimension=0, tiled=True),
    )
    home_out, home_dx = (
        lax.all_to_all(
            summed_out[0].astype(jnp.bfloat16), "expert", split_axis=0, concat_axis=0, tiled=True
        ),
        lax.all_to_all(
            summed_dx[0].astype(jnp.bfloat16), "expert", split_axis=0, concat_axis=0, tiled=True
        ),
    )
    out_pairs = (
        home_out.reshape(owners * capacity, feature_width)[slot_of]
        .reshape(tok_rows, top_count, feature_width)
        .astype(jnp.float32)
    )
    dx_pairs = (
        home_dx.reshape(owners * capacity, feature_width)[slot_of]
        .reshape(tok_rows, top_count, feature_width)
        .astype(jnp.float32)
    )
    mixed_out = jnp.sum(gates[:, :, None] * out_pairs, axis=1).astype(jnp.bfloat16)
    d_gates = jnp.sum(upstream.astype(jnp.float32)[:, None, :] * out_pairs, axis=2)
    d_tokens = jnp.sum(dx_pairs, axis=1).astype(jnp.bfloat16)
    return (
        mixed_out,
        d_tokens,
        d_gates,
        grad_up.astype(jnp.bfloat16)[None],
        grad_down.astype(jnp.bfloat16)[None],
    )


def swapped(array, bit):
    return lax.ppermute(array, "expert", tuple(((i, i ^ bit) for i in range(16))))


def shifted(array, step, senders):
    return lax.ppermute(
        array,
        "expert",
        tuple(((i, i + 4 * step) for z in senders for i in range(4 * z, 4 * z + 4))),
    )


def add_rows(first, *others):
    total = first.astype(jnp.float32)
    for other in others:
        total = total + other.astype(jnp.float32)
    return total.astype(jnp.bfloat16)


def gathered_slots(block, layer, first, second):
    up_one = shifted(block, 1, (0, 1, 2))
    down_one = shifted(block, -1, (3, 2, 1))
    up_two = shifted(up_one, 1, (1, 2))
    down_two = shifted(down_one, -1, (2, 1))
    up_three = shifted(up_two, 1, (2,))
    down_three = shifted(down_two, -1, (1,))
    low = layer < 2
    far = jnp.where(
        low, jnp.where(layer == 0, down_three, up_one), jnp.where(layer == 3, up_three, down_one)
    )
    columns = (block, jnp.where(low, down_one, up_one), jnp.where(low, down_two, up_two), far)
    slots = []
    for column in columns:
        pair = jnp.stack([column, swapped(column, first)])
        other = swapped(pair, second)
        if first == 1:
            slots.append(jnp.concatenate([pair[0], pair[1], other[0], other[1]], axis=0))
        else:
            slots.append(jnp.concatenate([pair[0], other[0], pair[1], other[1]], axis=0))
    return slots


def scattered_column(rows, tok_rows, first, second):
    blocks = [rows[i * tok_rows : (i + 1) * tok_rows].astype(jnp.bfloat16) for i in range(4)]
    kept, sent = ((0, 1), (2, 3)) if first == 2 else ((0, 2), (1, 3))
    came = swapped(jnp.stack([blocks[i] for i in sent]), first)
    near = add_rows(blocks[kept[0]], came[0])
    far = add_rows(blocks[kept[1]], came[1])
    return add_rows(near, swapped(far, second))


def scattered_layers(columns, layer):
    up = shifted(columns[3], 1, (0,))
    down = shifted(columns[3], -1, (3,))
    up = shifted(add_rows(columns[2], up), 1, (0, 1))
    down = shifted(add_rows(columns[2], down), -1, (3, 2))
    up = shifted(add_rows(jnp.where(layer == 2, columns[3], columns[1]), up), 1, (0, 1, 2))
    down = shifted(add_rows(jnp.where(layer == 1, columns[3], columns[1]), down), -1, (3, 2, 1))
    return add_rows(columns[0], up, down)


def transposed_dot(rows, weights):
    return lax.dot_general(
        rows, weights, (((1,), (1,)), ((), ())), preferred_element_type=jnp.float32
    )


def outer(rows, columns):
    return lax.dot_general(
        rows, columns, (((0,), (0,)), ((), ())), preferred_element_type=jnp.float32
    )


def dense_shards(tokens, routes, gates, upstream, w_up, w_down):
    tok_rows, width = tokens.shape
    owners = lax.axis_size("expert")
    half = w_up.shape[2]
    swap = ((0, 1), (1, 0))
    mine = lax.axis_index("expert")
    layer = mine // 4
    up_local, down_local = (w_up[0], w_down[0])
    named = routes[:, :, None] == jnp.arange(owners, dtype=jnp.int32)
    gate_of = jnp.sum(jnp.where(named, gates[:, :, None], 0.0), axis=1)
    gate_all = lax.all_gather(gate_of, "expert", axis=0, tiled=True).reshape(
        owners, tok_rows, owners
    )
    gate_mine = lax.dynamic_index_in_dim(gate_all, mine, axis=2, keepdims=False)
    layers = (
        layer,
        jnp.where(layer < 2, layer + 1, layer - 1),
        jnp.where(layer < 2, layer + 2, layer - 2),
        jnp.where(layer % 2 == 0, 3, 0),
    )
    sources = [jnp.stack([z * 4 + (mine % 4 ^ flip) for flip in range(4)]) for z in layers]
    slots_x = gathered_slots(tokens, layer, 1, 2)
    slots_u = gathered_slots(upstream, layer, 2, 1)
    up_full = jnp.concatenate([up_local, lax.ppermute(up_local, "tok", swap)], axis=1)
    down_full = jnp.concatenate([down_local, lax.ppermute(down_local, "tok", swap)], axis=0)
    gated, slopes, inners = ([None] * 4, [None] * 4, [None] * 4)
    mixed_columns, dx_columns = ([None] * 4, [None] * 4)
    for s in range(4):
        gate = gate_mine[sources[s]].reshape(-1)[:, None]
        hidden = jnp.dot(slots_x[s], up_full, preferred_element_type=jnp.float32)
        value = gelu_value(hidden)
        gated[s] = (gate * value).astype(jnp.bfloat16)
        back = transposed_dot(slots_u[s], down_full)
        inners[s] = jnp.sum(value * back, axis=1).reshape(4, tok_rows)
        slopes[s] = (gate * back * gelu_slope(hidden)).astype(jnp.bfloat16)
    for s in (3, 2, 1, 0):
        out_part = jnp.dot(gated[s], down_full, preferred_element_type=jnp.float32)
        mixed_columns[s] = scattered_column(out_part, tok_rows, 2, 1)
        dx_part = transposed_dot(slopes[s], up_full)
        dx_columns[s] = scattered_column(dx_part, tok_rows, 1, 2)
    mixed = scattered_layers(mixed_columns, layer)
    d_tokens = scattered_layers(dx_columns, layer)
    order = jnp.concatenate(sources)
    inner = jnp.zeros((owners, tok_rows), jnp.float32).at[order].set(jnp.concatenate(inners))
    inner_all = lax.all_gather(inner, "expert", axis=0, tiled=True).reshape(
        owners, owners, tok_rows
    )
    home = lax.dynamic_index_in_dim(inner_all, mine, axis=1, keepdims=False)
    d_gates = jnp.sum(jnp.where(named, home.T[:, None, :], 0.0), axis=2)
    all_x, all_u = (jnp.concatenate(slots_x), jnp.concatenate(slots_u))
    act, d_hidden = (jnp.concatenate(gated), jnp.concatenate(slopes))
    down_far = outer(act[:, half:], all_u).astype(jnp.bfloat16)
    up_far = outer(all_x, d_hidden[:, half:]).astype(jnp.bfloat16)
    down_near = outer(act[:, :half], all_u)
    up_near = outer(all_x, d_hidden[:, :half])
    grad_down = down_near + lax.ppermute(down_far, "tok", swap).astype(jnp.float32)
    grad_up = up_near + lax.ppermute(up_far, "tok", swap).astype(jnp.float32)
    return (
        mixed,
        d_tokens,
        d_gates,
        grad_up.astype(jnp.bfloat16)[None],
        grad_down.astype(jnp.bfloat16)[None],
    )


def shards(tokens, routes, gates, upstream, w_up, w_down):
    dense = lax.axis_size("expert") == 16 and lax.axis_size("tok") == 2
    body = dense_shards if dense else routed_shards
    return body(tokens, routes, gates, upstream, w_up, w_down)


def solution(mesh):
    return jax.shard_map(
        shards,
        mesh=mesh,
        in_specs=(
            P(("expert", "tok"), None),
            P(("expert", "tok"), None),
            P(("expert", "tok"), None),
            P(("expert", "tok"), None),
            P("expert", None, "tok"),
            P("expert", "tok", None),
        ),
        out_specs=(
            P(("expert", "tok"), None),
            P(("expert", "tok"), None),
            P(("expert", "tok"), None),
            P("expert", None, "tok"),
            P("expert", "tok", None),
        ),
        check_vma=False,
    )
```

profile of v0, /device:TPU:20, one launch (start us, length us, event | category | flops | bytes accessed | tf_op | source)
XLA Modules:
  0.0 542.9 jit_solution(3025906620837556485)
XLA Ops:
  18.8 5.5 %collective-permute-done.30 = bf16[64,3584]{1,0:T(8,128)(2,1)S(1)} collective-permute-done((bf16[64,3584]{1,0:T(8,128)(2,1)}, bf16[64,3584]{1,0:T(8,128)(2,1)S(1)}, u32[]{:S(2)}, u32[]{:S(2)}) %collective-permute-start.30) | collective-permute-done | bytes 458784 | tf_op jit(solution)/shard_map/ppermute | solution.py:112
  27.9 13.7 %collective-permute-done.1 = bf16[2,64,3584]{2,1,0:T(8,128)(2,1)S(1)} collective-permute-done((bf16[2,64,3584]{2,1,0:T(8,128)(2,1)S(1)}, bf16[2,64,3584]{2,1,0:T(8,128)(2,1)S(1)}, u32[]{:S(2)}, u32[]{:S(2)}) %collective-permute-start.1) | collective-permute-done | bytes 917536 | tf_op jit(solution)/shard_map/ppermute | solution.py:112
  43.8 17.9 %collective-permute-done.31 = bf16[2,64,3584]{2,1,0:T(8,128)(2,1)S(1)} collective-permute-done((bf16[2,64,3584]{2,1,0:T(8,128)(2,1)S(1)}, bf16[2,64,3584]{2,1,0:T(8,128)(2,1)S(1)}, u32[]{:S(2)}, u32[]{:S(2)}) %collective-permute-start.31) | collective-permute-done | bytes 917536 | tf_op jit(solution)/shard_map/ppermute | solution.py:112
  71.0 9.9 %collective-permute-done.16 = bf16[64,3584]{1,0:T(8,128)(2,1)S(1)} collective-permute-done((bf16[64,3584]{1,0:T(8,128)(2,1)S(1)}, bf16[64,3584]{1,0:T(8,128)(2,1)S(1)}, u32[]{:S(2)}, u32[]{:S(2)}) %collective-permute-start.16) | collective-permute-done | bytes 458784 | tf_op jit(solution)/shard_map/ppermute | solution.py:112
  84.6 17.6 %collective-permute-done.17 = bf16[2,64,3584]{2,1,0:T(8,128)(2,1)S(1)} collective-permute-done((bf16[2,64,3584]{2,1,0:T(8,128)(2,1)S(1)}, bf16[2,64,3584]{2,1,0:T(8,128)(2,1)S(1)}, u32[]{:S(2)}, u32[]{:S(2)}) %collective-permute-start.17) | collective-permute-done | bytes 917536 | tf_op jit(solution)/shard_map/ppermute | solution.py:112
  104.9 17.5 %collective-permute-done.45 = bf16[2,64,3584]{2,1,0:T(8,128)(2,1)S(1)} collective-permute-done((bf16[2,64,3584]{2,1,0:T(8,128)(2,1)S(1)}, bf16[2,64,3584]{2,1,0:T(8,128)(2,1)S(1)}, u32[]{:S(2)}, u32[]{:S(2)}) %collective-permute-start.45) | collective-permute-done | bytes 917536 | tf_op jit(solution)/shard_map/ppermute | solution.py:112
  135.2 4.6 collective-permute-done.38
  143.7 4.6 collective-permute-done.20
  150.6 6.1 %collective-permute-done.48 = bf16[64,3584]{1,0:T(8,128)(2,1)S(1)} collective-permute-done((bf16[64,3584]{1,0:T(8,128)(2,1)S(1)}, bf16[64,3584]{1,0:T(8,128)(2,1)S(1)}, u32[]{:S(2)}, u32[]{:S(2)}) %collective-permute-start.48) | collective-permute-done | bytes 458784 | tf_op jit(solution)/shard_map/ppermute | solution.py:112
  159.2 5.4 collective-permute-start.39
  173.6 6.8 %multiply_reduce_fusion.2 = (f32[256]{0:T(256)S(1)}, f32[256,1024]{1,0:T(8,128)}) fusion(f32[256,1024]{1,0:T(8,128)} %fusion.18, bf16[512,3584]{1,0:T(8,128)(2,1)} %copy-done.39, bf16[512,3584]{1,0:T(8,128)(2,1)} %bitcast.290, bf16[64,3584]{1,0:T(8,128)(2,1)} %get-tuple-element.58, bf16[64,3584]{1,0:T(8,128)(2,1)S(1)} %collective-permute-done.44, ...), kind=kOutput, calls=%fused_computation.133 | convolution fusion | flops 1903689472 | bytes 11273216 | tf_op jit(solution)/shard_map/dot_general | solution.py:173
  186.5 11.9 %collective-permute-done.49 = bf16[2,64,3584]{2,1,0:T(8,128)(2,1)S(1)} collective-permute-done((bf16[2,64,3584]{2,1,0:T(8,128)(2,1)}, bf16[2,64,3584]{2,1,0:T(8,128)(2,1)S(1)}, u32[]{:S(2)}, u32[]{:S(2)}) %collective-permute-start.49) | collective-permute-done | bytes 917536 | tf_op jit(solution)/shard_map/ppermute | solution.py:112
  211.7 5.0 collective-permute-done.40
  220.1 6.6 %collective-permute-done.13 = bf16[2,64,3584]{2,1,0:T(8,128)(2,1)S(1)} collective-permute-done((bf16[2,64,3584]{2,1,0:T(8,128)(2,1)S(1)}, bf16[2,64,3584]{2,1,0:T(8,128)(2,1)S(1)}, u32[]{:S(2)}, u32[]{:S(2)}) %collective-permute-start.13) | collective-permute-done | bytes 917536 | tf_op jit(solution)/shard_map/ppermute | solution.py:112
  238.4 33.8 %all_gather.7 = f32[256,64]{1,0:T(8,128)S(1)} all-gather(f32[16,64]{1,0:T(8,128)S(1)} %scatter_custom_fusion), channel_id=1, replica_groups=mesh['expert'=16,'tok'=2] {'expert'}, dimensions={0}, use_global_device_ids=true | all-gather | bytes 69632 | tf_op jit(solution)/shard_map/all_gather | solution.py:228
  272.8 33.2 %all-gather = f32[16,64,16]{1,2,0:T(8,128)S(1)} all-gather(f32[1,64,16]{1,2,0:T(8,128)S(1)} %bitcast.279), channel_id=1, replica_groups=mesh['expert'=16,'tok'=2] {'expert'}, dimensions={0}, use_global_device_ids=true | all-gather | bytes 69632 | tf_op jit(solution)/shard_map/all_gather | solution.py:194
  310.9 5.3 convolution_convert_fusion.5
  328.6 5.3 convolution_convert_fusion.4
  334.0 5.3 convolution_convert_fusion.2
  341.7 4.3 convolution_convert_fusion.9
  350.6 5.2 convolution_convert_fusion.8
  355.9 5.2 convolution_convert_fusion.6
  364.1 8.6 %convolution_convert_fusion = bf16[512,3584]{1,0:T(8,128)(2,1)} fusion(bf16[1024,3584]{1,0:T(8,128)(2,1)} %constant_dynamic-update-slice_fusion.16, bf16[1024,1024]{1,0:T(8,128)(2,1)S(1)} %pad_maximum_fusion.3), kind=kOutput, calls=%fused_computation.9 | convolution fusion | flops 3759931392 | bytes 12058624 | tf_op jit(solution)/shard_map/dot_general | solution.py:179
  374.2 8.6 %convolution_convert_fusion.1 = bf16[3584,512]{1,0:T(8,128)(2,1)} fusion(bf16[1024,3584]{1,0:T(8,128)(2,1)} %constant_dynamic-update-slice_fusion, bf16[1024,1024]{1,0:T(8,128)(2,1)S(1)} %pad_maximum_fusion.2), kind=kOutput, calls=%fused_computation.10 | convolution fusion | flops 3759931392 | bytes 12058624 | tf_op jit(solution)/shard_map/dot_general | solution.py:179
  392.3 10.4 %collective-permute-done.18 = bf16[2,64,3584]{2,1,0:T(8,128)(2,1)S(1)} collective-permute-done((bf16[2,64,3584]{2,1,0:T(8,128)(2,1)S(1)}, bf16[2,64,3584]{2,1,0:T(8,128)(2,1)S(1)}, u32[]{:S(2)}, u32[]{:S(2)}) %collective-permute-start.18) | collective-permute-done | bytes 917536 | tf_op jit(solution)/shard_map/ppermute | solution.py:112
  402.9 25.5 %collective-permute-done.14 = bf16[2,64,3584]{2,1,0:T(8,128)(2,1)S(1)} collective-permute-done((bf16[2,64,3584]{2,1,0:T(8,128)(2,1)S(1)}, bf16[2,64,3584]{2,1,0:T(8,128)(2,1)S(1)}, u32[]{:S(2)}, u32[]{:S(2)}) %collective-permute-start.14) | collective-permute-done | bytes 917536 | tf_op jit(solution)/shard_map/ppermute | solution.py:112
  429.2 12.3 %collective-permute-done.43 = bf16[64,3584]{1,0:T(8,128)(2,1)S(1)} collective-permute-done((bf16[64,3584]{1,0:T(8,128)(2,1)S(1)}, bf16[64,3584]{1,0:T(8,128)(2,1)S(1)}, u32[]{:S(2)}, u32[]{:S(2)}) %collective-permute-start.43) | collective-permute-done | bytes 458784 | tf_op jit(solution)/shard_map/ppermute | solution.py:112
  445.5 17.4 %collective-permute-done.55 = bf16[64,3584]{1,0:T(8,128)(2,1)S(1)} collective-permute-done((bf16[64,3584]{1,0:T(8,128)(2,1)S(1)}, bf16[64,3584]{1,0:T(8,128)(2,1)S(1)}, u32[]{:S(2)}, u32[]{:S(2)}) %collective-permute-start.55) | collective-permute-done | bytes 458784 | tf_op jit(solution)/shard_map/ppermute | solution.py:116
  465.3 12.5 %collective-permute-done.27 = bf16[64,3584]{1,0:T(8,128)(2,1)S(1)} collective-permute-done((bf16[64,3584]{1,0:T(8,128)(2,1)S(1)}, bf16[64,3584]{1,0:T(8,128)(2,1)S(1)}, u32[]{:S(2)}, u32[]{:S(2)}) %collective-permute-start.27) | collective-permute-done | bytes 458784 | tf_op jit(solution)/shard_map/ppermute | solution.py:116
  479.1 4.6 collective-permute-start.56
  525.1 8.9 %fusion = bf16[1,3584,512]{2,1,0:T(8,128)(2,1)} fusion(bf16[3584,512]{1,0:T(8,128)(2,1)S(1)} %collective-permute-done.58, bf16[1024,3584]{1,0:T(8,128)(2,1)} %constant_dynamic-update-slice_fusion, bf16[1024,1024]{1,0:T(8,128)(2,1)S(1)} %pad_maximum_fusion.2), kind=kOutput, calls=%fused_computation.11 | convolution fusion | flops 3763601408 | bytes 15728640 | tf_op jit(solution)/shard_map/dot_general | solution.py:179
  534.0 8.7 %fusion.1 = bf16[1,512,3584]{2,1,0:T(8,128)(2,1)} fusion(bf16[512,3584]{1,0:T(8,128)(2,1)S(1)} %collective-permute-done.59, bf16[1024,3584]{1,0:T(8,128)(2,1)} %constant_dynamic-update-slice_fusion.16, bf16[1024,1024]{1,0:T(8,128)(2,1)S(1)} %pad_maximum_fusion.3), kind=kOutput, calls=%fused_computation.12 | convolution fusion | flops 3763601408 | bytes 15728640 | tf_op jit(solution)/shard_map/dot_general | solution.py:179
  (312 shorter events, 192.6 us)
Async XLA Ops:
  0.6 62.7 %collective-permute-start.6 = (bf16[64,3584]{1,0:T(8,128)(2,1)}, bf16[64,3584]{1,0:T(8,128)(2,1)S(1)}, u32[]{:S(2)}, u32[]{:S(2)}) collective-permute-start(bf16[64,3584]{1,0:T(8,128)(2,1)} %param.6), channel_id=1, source_target_pairs={{24,16},{26,18},{28,20},{30,22},{16,8},{18,10},{20,12},{22,14},{8,... | collective-permute-start | bytes 1376264 | tf_op jit(solution)/shard_map/ppermute | solution.py:116
  4.7 59.2 %collective-permute-start.9 = (bf16[64,3584]{1,0:T(8,128)(2,1)}, bf16[64,3584]{1,0:T(8,128)(2,1)S(1)}, u32[]{:S(2)}, u32[]{:S(2)}) collective-permute-start(bf16[64,3584]{1,0:T(8,128)(2,1)} %param.6), channel_id=1, source_target_pairs={{0,8},{2,10},{4,12},{6,14},{8,16},{10,18},{12,20},{14,22},{16,24},... | collective-permute-start | bytes 1376264 | tf_op jit(solution)/shard_map/ppermute | solution.py:116
  8.2 60.5 %collective-permute-start.34 = (bf16[64,3584]{1,0:T(8,128)(2,1)}, bf16[64,3584]{1,0:T(8,128)(2,1)S(1)}, u32[]{:S(2)}, u32[]{:S(2)}) collective-permute-start(bf16[64,3584]{1,0:T(8,128)(2,1)} %param.9), channel_id=1, source_target_pairs={{24,16},{26,18},{28,20},{30,22},{16,8},{18,10},{20,12},{22,14},{8,... | collective-permute-start | bytes 1376264 | tf_op jit(solution)/shard_map/ppermute | solution.py:116
  16.5 25.1 %collective-permute-start.1 = (bf16[2,64,3584]{2,1,0:T(8,128)(2,1)S(1)}, bf16[2,64,3584]{2,1,0:T(8,128)(2,1)S(1)}, u32[]{:S(2)}, u32[]{:S(2)}) collective-permute-start(bf16[2,64,3584]{2,1,0:T(8,128)(2,1)S(1)} %pad_maximum_fusion.4), channel_id=1, source_target_pairs={{0,4},{2,6},{4,0},{6,2},{8,12},{10,14},{12,8},{14,10},{16,20},{18,... | collective-permute-start | bytes 2752520 | tf_op jit(solution)/shard_map/ppermute | solution.py:112
  24.3 45.0 %collective-permute-start.37 = (bf16[64,3584]{1,0:T(8,128)(2,1)S(1)}, bf16[64,3584]{1,0:T(8,128)(2,1)S(1)}, u32[]{:S(2)}, u32[]{:S(2)}) collective-permute-start(bf16[64,3584]{1,0:T(8,128)(2,1)S(1)} %copy-done.1), channel_id=1, source_target_pairs={{0,8},{2,10},{4,12},{6,14},{8,16},{10,18},{12,20},{14,22},{16,24},... | collective-permute-start | bytes 1376264 | tf_op jit(solution)/shard_map/ppermute | solution.py:116
  41.6 20.0 %collective-permute-start.31 = (bf16[2,64,3584]{2,1,0:T(8,128)(2,1)S(1)}, bf16[2,64,3584]{2,1,0:T(8,128)(2,1)S(1)}, u32[]{:S(2)}, u32[]{:S(2)}) collective-permute-start(bf16[2,64,3584]{2,1,0:T(8,128)(2,1)S(1)} %pad_maximum_fusion.12), channel_id=1, source_target_pairs={{0,2},{2,0},{4,6},{6,4},{8,10},{10,8},{12,14},{14,12},{16,18},{18,... | collective-permute-start | bytes 2752520 | tf_op jit(solution)/shard_map/ppermute | solution.py:112
  61.7 97.5 %collective-permute-start.2 = (bf16[3584,512]{1,0:T(8,128)(2,1)S(1)}, bf16[3584,512]{1,0:T(8,128)(2,1)S(1)}, u32[]{:S(2)}, u32[]{:S(2)}) collective-permute-start(bf16[3584,512]{1,0:T(8,128)(2,1)S(1)} %bitcast.284), channel_id=1, source_target_pairs={{0,1},{1,0},{2,3},{3,2},{4,5},{5,4},{6,7},{7,6},{8,9},{9,8},{10,11... | collective-permute-start | bytes 11010056 | tf_op jit(solution)/shard_map/ppermute | solution.py:207
  63.3 103.4 %collective-permute-start.3 = (bf16[512,3584]{1,0:T(8,128)(2,1)S(1)}, bf16[512,3584]{1,0:T(8,128)(2,1)S(1)}, u32[]{:S(2)}, u32[]{:S(2)}) collective-permute-start(bf16[512,3584]{1,0:T(8,128)(2,1)S(1)} %bitcast.293), channel_id=1, source_target_pairs={{0,1},{1,0},{2,3},{3,2},{4,5},{5,4},{6,7},{7,6},{8,9},{9,8},{10,11... | collective-permute-start | bytes 11010056 | tf_op jit(solution)/shard_map/ppermute | solution.py:208
  63.9 63.0 %collective-permute-start.7 = (bf16[64,3584]{1,0:T(8,128)(2,1)S(1)}, bf16[64,3584]{1,0:T(8,128)(2,1)}, u32[]{:S(2)}, u32[]{:S(2)}) collective-permute-start(bf16[64,3584]{1,0:T(8,128)(2,1)S(1)} %collective-permute-done.6), channel_id=1, source_target_pairs={{16,8},{18,10},{20,12},{22,14},{8,0},{10,2},{12,4},{14,6},{17,9},{... | collective-permute-start | bytes 1376264 | tf_op jit(solution)/shard_map/ppermute | solution.py:116
  81.0 21.2 %collective-permute-start.17 = (bf16[2,64,3584]{2,1,0:T(8,128)(2,1)S(1)}, bf16[2,64,3584]{2,1,0:T(8,128)(2,1)S(1)}, u32[]{:S(2)}, u32[]{:S(2)}) collective-permute-start(bf16[2,64,3584]{2,1,0:T(8,128)(2,1)S(1)} %pad_maximum_fusion.8), channel_id=1, source_target_pairs={{0,4},{2,6},{4,0},{6,2},{8,12},{10,14},{12,8},{14,10},{16,20},{18,... | collective-permute-start | bytes 2752520 | tf_op jit(solution)/shard_map/ppermute | solution.py:112
  82.4 46.4 %collective-permute-start.10 = (bf16[64,3584]{1,0:T(8,128)(2,1)S(1)}, bf16[64,3584]{1,0:T(8,128)(2,1)}, u32[]{:S(2)}, u32[]{:S(2)}) collective-permute-start(bf16[64,3584]{1,0:T(8,128)(2,1)S(1)} %copy-done.15), channel_id=1, source_target_pairs={{8,16},{10,18},{12,20},{14,22},{16,24},{18,26},{20,28},{22,30},{9,... | collective-permute-start | bytes 1376264 | tf_op jit(solution)/shard_map/ppermute | solution.py:116
  102.2 20.2 %collective-permute-start.45 = (bf16[2,64,3584]{2,1,0:T(8,128)(2,1)S(1)}, bf16[2,64,3584]{2,1,0:T(8,128)(2,1)S(1)}, u32[]{:S(2)}, u32[]{:S(2)}) collective-permute-start(bf16[2,64,3584]{2,1,0:T(8,128)(2,1)S(1)} %pad_maximum_fusion.16), channel_id=1, source_target_pairs={{0,2},{2,0},{4,6},{6,4},{8,10},{10,8},{12,14},{14,12},{16,18},{18,... | collective-permute-start | bytes 2752520 | tf_op jit(solution)/shard_map/ppermute | solution.py:112
  128.8 54.3 %collective-permute-start.8 = (bf16[64,3584]{1,0:T(8,128)(2,1)}, bf16[64,3584]{1,0:T(8,128)(2,1)}, u32[]{:S(2)}, u32[]{:S(2)}) collective-permute-start(bf16[64,3584]{1,0:T(8,128)(2,1)} %collective-permute-done.7), channel_id=1, source_target_pairs={{8,0},{10,2},{12,4},{14,6},{9,1},{11,3},{13,5},{15,7}} | collective-permute-start | bytes 1376264 | tf_op jit(solution)/shard_map/ppermute | solution.py:116
  133.1 50.0 %collective-permute-start.11 = (bf16[64,3584]{1,0:T(8,128)(2,1)}, bf16[64,3584]{1,0:T(8,128)(2,1)}, u32[]{:S(2)}, u32[]{:S(2)}) collective-permute-start(bf16[64,3584]{1,0:T(8,128)(2,1)} %collective-permute-done.10), channel_id=1, source_target_pairs={{16,24},{18,26},{20,28},{22,30},{17,25},{19,27},{21,29},{23,31}} | collective-permute-start | bytes 1376264 | tf_op jit(solution)/shard_map/ppermute | solution.py:116
  156.7 46.3 %collective-permute-start.36 = (bf16[64,3584]{1,0:T(8,128)(2,1)}, bf16[64,3584]{1,0:T(8,128)(2,1)}, u32[]{:S(2)}, u32[]{:S(2)}) collective-permute-start(bf16[64,3584]{1,0:T(8,128)(2,1)} %collective-permute-done.35), channel_id=1, source_target_pairs={{8,0},{10,2},{12,4},{14,6},{9,1},{11,3},{13,5},{15,7}} | collective-permute-start | bytes 1376264 | tf_op jit(solution)/shard_map/ppermute | solution.py:116
  159.2 43.9 %collective-permute-start.39 = (bf16[64,3584]{1,0:T(8,128)(2,1)}, bf16[64,3584]{1,0:T(8,128)(2,1)}, u32[]{:S(2)}, u32[]{:S(2)}) collective-permute-start(bf16[64,3584]{1,0:T(8,128)(2,1)} %collective-permute-done.38), channel_id=1, source_target_pairs={{16,24},{18,26},{20,28},{22,30},{17,25},{19,27},{21,29},{23,31}} | collective-permute-start | bytes 1376264 | tf_op jit(solution)/shard_map/ppermute | solution.py:116
  185.5 24.3 %collective-permute-start.12 = (bf16[64,3584]{1,0:T(8,128)(2,1)}, bf16[64,3584]{1,0:T(8,128)(2,1)S(1)}, u32[]{:S(2)}, u32[]{:S(2)}) collective-permute-start(bf16[64,3584]{1,0:T(8,128)(2,1)} %get-tuple-element.14), channel_id=1, source_target_pairs={{0,2},{2,0},{4,6},{6,4},{8,10},{10,8},{12,14},{14,12},{16,18},{18,... | collective-permute-start | bytes 1376264 | tf_op jit(solution)/shard_map/ppermute | solution.py:112
  316.4 66.4 %collective-permute-start.32 = (bf16[2,64,3584]{2,1,0:T(8,128)(2,1)S(1)}, bf16[2,64,3584]{2,1,0:T(8,128)(2,1)}, u32[]{:S(2)}, u32[]{:S(2)}) collective-permute-start(bf16[2,64,3584]{2,1,0:T(8,128)(2,1)S(1)} %pad_maximum_fusion.13), channel_id=1, source_target_pairs={{0,2},{2,0},{4,6},{6,4},{8,10},{10,8},{12,14},{14,12},{16,18},{18,... | collective-permute-start | bytes 2752520 | tf_op jit(solution)/shard_map/ppermute | solution.py:112
  325.2 60.8 %collective-permute-start.46 = (bf16[2,64,3584]{2,1,0:T(8,128)(2,1)}, bf16[2,64,3584]{2,1,0:T(8,128)(2,1)}, u32[]{:S(2)}, u32[]{:S(2)}) collective-permute-start(bf16[2,64,3584]{2,1,0:T(8,128)(2,1)} %pad_maximum_fusion.17), channel_id=1, source_target_pairs={{0,2},{2,0},{4,6},{6,4},{8,10},{10,8},{12,14},{14,12},{16,18},{18,... | collective-permute-start | bytes 2752520 | tf_op jit(solution)/shard_map/ppermute | solution.py:112
  339.4 47.9 %collective-permute-start.50 = (bf16[2,64,3584]{2,1,0:T(8,128)(2,1)S(1)}, bf16[2,64,3584]{2,1,0:T(8,128)(2,1)S(1)}, u32[]{:S(2)}, u32[]{:S(2)}) collective-permute-start(bf16[2,64,3584]{2,1,0:T(8,128)(2,1)S(1)} %pad_maximum_fusion.19), channel_id=1, source_target_pairs={{0,2},{2,0},{4,6},{6,4},{8,10},{10,8},{12,14},{14,12},{16,18},{18,... | collective-permute-start | bytes 2752520 | tf_op jit(solution)/shard_map/ppermute | solution.py:112
  340.1 49.3 %collective-permute-start.42 = (bf16[2,64,3584]{2,1,0:T(8,128)(2,1)S(1)}, bf16[2,64,3584]{2,1,0:T(8,128)(2,1)}, u32[]{:S(2)}, u32[]{:S(2)}) collective-permute-start(bf16[2,64,3584]{2,1,0:T(8,128)(2,1)S(1)} %pad_maximum_fusion.15), channel_id=1, source_target_pairs={{0,2},{2,0},{4,6},{6,4},{8,10},{10,8},{12,14},{14,12},{16,18},{18,... | collective-permute-start | bytes 2752520 | tf_op jit(solution)/shard_map/ppermute | solution.py:112
  346.1 44.5 %collective-permute-start.4 = (bf16[2,64,3584]{2,1,0:T(8,128)(2,1)S(1)}, bf16[2,64,3584]{2,1,0:T(8,128)(2,1)}, u32[]{:S(2)}, u32[]{:S(2)}) collective-permute-start(bf16[2,64,3584]{2,1,0:T(8,128)(2,1)S(1)} %pad_maximum_fusion.5), channel_id=1, source_target_pairs={{0,4},{2,6},{4,0},{6,2},{8,12},{10,14},{12,8},{14,10},{16,20},{18,... | collective-permute-start | bytes 2752520 | tf_op jit(solution)/shard_map/ppermute | solution.py:112
  382.8 20.0 %collective-permute-start.18 = (bf16[2,64,3584]{2,1,0:T(8,128)(2,1)S(1)}, bf16[2,64,3584]{2,1,0:T(8,128)(2,1)S(1)}, u32[]{:S(2)}, u32[]{:S(2)}) collective-permute-start(bf16[2,64,3584]{2,1,0:T(8,128)(2,1)S(1)} %pad_maximum_fusion.9), channel_id=1, source_target_pairs={{0,4},{2,6},{4,0},{6,2},{8,12},{10,14},{12,8},{14,10},{16,20},{18,... | collective-permute-start | bytes 2752520 | tf_op jit(solution)/shard_map/ppermute | solution.py:112
  386.0 42.6 %collective-permute-start.22 = (bf16[2,64,3584]{2,1,0:T(8,128)(2,1)S(1)}, bf16[2,64,3584]{2,1,0:T(8,128)(2,1)S(1)}, u32[]{:S(2)}, u32[]{:S(2)}) collective-permute-start(bf16[2,64,3584]{2,1,0:T(8,128)(2,1)S(1)} %pad_maximum_fusion.11), channel_id=1, source_target_pairs={{0,4},{2,6},{4,0},{6,2},{8,12},{10,14},{12,8},{14,10},{16,20},{18,... | collective-permute-start | bytes 2752520 | tf_op jit(solution)/shard_map/ppermute | solution.py:112
  387.3 41.1 %collective-permute-start.14 = (bf16[2,64,3584]{2,1,0:T(8,128)(2,1)S(1)}, bf16[2,64,3584]{2,1,0:T(8,128)(2,1)S(1)}, u32[]{:S(2)}, u32[]{:S(2)}) collective-permute-start(bf16[2,64,3584]{2,1,0:T(8,128)(2,1)S(1)} %pad_maximum_fusion.7), channel_id=1, source_target_pairs={{0,4},{2,6},{4,0},{6,2},{8,12},{10,14},{12,8},{14,10},{16,20},{18,... | collective-permute-start | bytes 2752520 | tf_op jit(solution)/shard_map/ppermute | solution.py:112
  389.4 135.7 %collective-permute-start.58 = (bf16[3584,512]{1,0:T(8,128)(2,1)S(1)}, bf16[3584,512]{1,0:T(8,128)(2,1)S(1)}, u32[]{:S(2)}, u32[]{:S(2)}) collective-permute-start(bf16[3584,512]{1,0:T(8,128)(2,1)S(1)} %copy-done.45), channel_id=1, source_target_pairs={{0,1},{1,0},{2,3},{3,2},{4,5},{5,4},{6,7},{7,6},{8,9},{9,8},{10,11... | collective-permute-start | bytes 11010056 | tf_op jit(solution)/shard_map/ppermute | solution.py:240
  390.6 143.3 %collective-permute-start.59 = (bf16[512,3584]{1,0:T(8,128)(2,1)}, bf16[512,3584]{1,0:T(8,128)(2,1)S(1)}, u32[]{:S(2)}, u32[]{:S(2)}) collective-permute-start(bf16[512,3584]{1,0:T(8,128)(2,1)} %convolution_convert_fusion), channel_id=1, source_target_pairs={{0,1},{1,0},{2,3},{3,2},{4,5},{5,4},{6,7},{7,6},{8,9},{9,8},{10,11... | collective-permute-start | bytes 11010056 | tf_op jit(solution)/shard_map/ppermute | solution.py:239
  402.8 42.1 %collective-permute-start.51 = (bf16[64,3584]{1,0:T(8,128)(2,1)S(1)}, bf16[64,3584]{1,0:T(8,128)(2,1)S(1)}, u32[]{:S(2)}, u32[]{:S(2)}) collective-permute-start(bf16[64,3584]{1,0:T(8,128)(2,1)S(1)} %fusion.102), channel_id=1, source_target_pairs={{0,4},{2,6},{4,0},{6,2},{8,12},{10,14},{12,8},{14,10},{16,20},{18,... | collective-permute-start | bytes 1376264 | tf_op jit(solution)/shard_map/ppermute | solution.py:112
  442.7 20.2 %collective-permute-start.55 = (bf16[64,3584]{1,0:T(8,128)(2,1)S(1)}, bf16[64,3584]{1,0:T(8,128)(2,1)S(1)}, u32[]{:S(2)}, u32[]{:S(2)}) collective-permute-start(bf16[64,3584]{1,0:T(8,128)(2,1)S(1)} %add_convert_fusion.7), channel_id=1, source_target_pairs={{24,16},{26,18},{28,20},{30,22},{25,17},{27,19},{29,21},{31,23}} | collective-permute-start | bytes 1376264 | tf_op jit(solution)/shard_map/ppermute | solution.py:116
  444.0 20.2 %collective-permute-start.52 = (bf16[64,3584]{1,0:T(8,128)(2,1)S(1)}, bf16[64,3584]{1,0:T(8,128)(2,1)S(1)}, u32[]{:S(2)}, u32[]{:S(2)}) collective-permute-start(bf16[64,3584]{1,0:T(8,128)(2,1)S(1)} %add_convert_fusion.7), channel_id=1, source_target_pairs={{0,8},{2,10},{4,12},{6,14},{1,9},{3,11},{5,13},{7,15}} | collective-permute-start | bytes 1376264 | tf_op jit(solution)/shard_map/ppermute | solution.py:116
  444.9 20.3 %collective-permute-start.23 = (bf16[64,3584]{1,0:T(8,128)(2,1)S(1)}, bf16[64,3584]{1,0:T(8,128)(2,1)S(1)}, u32[]{:S(2)}, u32[]{:S(2)}) collective-permute-start(bf16[64,3584]{1,0:T(8,128)(2,1)S(1)} %fusion.110), channel_id=1, source_target_pairs={{0,2},{2,0},{4,6},{6,4},{8,10},{10,8},{12,14},{14,12},{16,18},{18,... | collective-permute-start | bytes 1376264 | tf_op jit(solution)/shard_map/ppermute | solution.py:112
  465.2 18.8 %collective-permute-start.47 = (bf16[64,3584]{1,0:T(8,128)(2,1)S(1)}, bf16[64,3584]{1,0:T(8,128)(2,1)S(1)}, u32[]{:S(2)}, u32[]{:S(2)}) collective-permute-start(bf16[64,3584]{1,0:T(8,128)(2,1)S(1)} %fusion.104), channel_id=1, source_target_pairs={{0,4},{2,6},{4,0},{6,2},{8,12},{10,14},{12,8},{14,10},{16,20},{18,... | collective-permute-start | bytes 1376264 | tf_op jit(solution)/shard_map/ppermute | solution.py:112
  (74 other events, 1021.1 us)
where the time goes:
time: 548 us; the launch traced here: 543 us
  waiting for transfers between devices  226 us (41%)
  matrix products  101 us (18%)
  starting transfers between devices  82.1 us (15%)
  blocking collectives  67 us (12%)
  other arithmetic  35.1 us (6%)
  local copies, waits for them, and re-layouts  30.5 us (6%)
    ppermute x32, waiting for transfers between devices, swapped(): lax.ppermute(array, 'expert', tuple(((i, i ^ bit) for i in range(16))))  169 us
    ppermute x24, waiting for transfers between devices, shifted(): lax.ppermute(array, 'expert', tuple(((i, i + 4 * step) for z in senders f...  56.8 us
    ppermute x24, starting transfers between devices, shifted(): lax.ppermute(array, 'expert', tuple(((i, i + 4 * step) for z in senders f...  53.6 us
    dot_general x8, matrix products, transposed_dot(): lax.dot_general(rows, weights, (((1,), (1,)), ((), ())), preferred_elemen...  36.7 us
    dot_general x4, matrix products, outer(): lax.dot_general(rows, columns, (((0,), (0,)), ((), ())), preferred_elemen...  34.7 us
    all_gather x1, blocking collectives, dense_shards(): lax.all_gather(inner, 'expert', axis=0, tiled=True)  33.8 us
    all_gather x1, blocking collectives, dense_shards(): lax.all_gather(gate_of, 'expert', axis=0, tiled=True)  33.2 us
    ppermute x32, starting transfers between devices, swapped(): lax.ppermute(array, 'expert', tuple(((i, i ^ bit) for i in range(16))))  27.2 us
  transfers between devices with their start and end apart: 60, of which 27 were waited for; matrix products, arithmetic and copies ran while one was open for 25% of the time, Pallas kernels for 0%

commit v1 on v0

--- a/solution.py
+++ b/solution.py
@@ -5,6 +5,18 @@
 
 GELU_C = 0.7978845608028654
 GELU_A = 0.044715
+
+
+def collect(x, axis, dim):
+    ways, here = (lax.axis_size(axis), lax.axis_index(axis))
+    grown, reach = (x, 1)
+    while reach < ways:
+        theirs = lax.ppermute(grown, axis, [(d, d ^ reach) for d in range(ways)])
+        mine_first = jnp.concatenate([grown, theirs], axis=dim)
+        theirs_first = jnp.concatenate([theirs, grown], axis=dim)
+        grown = jnp.where(here & reach == 0, mine_first, theirs_first)
+        reach = 2 * reach
+    return grown
 
 
 def gelu_value(hidden):
@@ -225,9 +237,7 @@
     d_tokens = scattered_layers(dx_columns, layer)
     order = jnp.concatenate(sources)
     inner = jnp.zeros((owners, tok_rows), jnp.float32).at[order].set(jnp.concatenate(inners))
-    inner_all = lax.all_gather(inner, "expert", axis=0, tiled=True).reshape(
-        owners, owners, tok_rows
-    )
+    inner_all = collect(inner, "expert", 0).reshape(owners, owners, tok_rows)
     home = lax.dynamic_index_in_dim(inner_all, mine, axis=1, keepdims=False)
     d_gates = jnp.sum(jnp.where(named, home.T[:, None, :], 0.0), axis=2)
     all_x, all_u = (jnp.concatenate(slots_x), jnp.concatenate(slots_u))

time: 548 us -> 525 us (0.958)
  blocking collectives: 67 us -> 33.3 us
  waiting for transfers between devices: 226 us -> 235 us
  starting transfers between devices: 82.1 us -> 91 us
  other arithmetic: 35.1 us -> 28.8 us
    all_gather x1 -> x0, blocking collectives: 33.8 us -> none  [dense_shards(): lax.all_gather(inner, 'expert', axis=0, tiled=True)]
    ppermute x0 -> x4, starting transfers between devices: none -> 7.23 us  [collect(): theirs = lax.ppermute(grown, axis, [(d, d ^ reach) for d in range(ways)])]
    ppermute x32, waiting for transfers between devices: 169 us -> 176 us  [swapped(): lax.ppermute(array, 'expert', tuple(((i, i ^ bit) for i in range(16))))]
    ppermute x0 -> x4, waiting for transfers between devices: none -> 6.55 us  [collect(): theirs = lax.ppermute(grown, axis, [(d, d ^ reach) for d in range(ways)])]
  transfers between devices with their start and end apart: 60 -> 64, of which waited for: 27 -> 32; matrix products, arithmetic and copies ran while one was open for 25% -> 25% of each run, Pallas kernels for 0% -> 0%
where the time goes in v1:
time: 525 us; the launch traced here: 520 us
  waiting for transfers between devices  235 us (45%)
  matrix products  97.5 us (19%)
  starting transfers between devices  91 us (17%)
  blocking collectives  33.3 us (6%)
  local copies, waits for them, and re-layouts  32.6 us (6%)
  other arithmetic  28.8 us (5%)
    ppermute x32, waiting for transfers between devices, swapped(): lax.ppermute(array, 'expert', tuple(((i, i ^ bit) for i in range(16))))  176 us
    ppermute x24, starting transfers between devices, shifted(): lax.ppermute(array, 'expert', tuple(((i, i + 4 * step) for z in senders f...  54.1 us
    ppermute x24, waiting for transfers between devices, shifted(): lax.ppermute(array, 'expert', tuple(((i, i + 4 * step) for z in senders f...  52.9 us
    dot_general x8, matrix products, transposed_dot(): lax.dot_general(rows, weights, (((1,), (1,)), ((), ())), preferred_elemen...  36.5 us
    all_gather x1, blocking collectives, dense_shards(): lax.all_gather(gate_of, 'expert', axis=0, tiled=True)  33.3 us
    dot_general x4, matrix products, outer(): lax.dot_general(rows, columns, (((0,), (0,)), ((), ())), preferred_elemen...  32.9 us
    ppermute x32, starting transfers between devices, swapped(): lax.ppermute(array, 'expert', tuple(((i, i ^ bit) for i in range(16))))  28.5 us
    unnamed x116, local copies, waits for them, and re-layouts  26 us
  transfers between devices with their start and end apart: 64, of which 32 were waited for; matrix products, arithmetic and copies ran while one was open for 25% of the time, Pallas kernels for 0%

profile of v1, /device:TPU:20, one launch (start us, length us, event | category | flops | bytes accessed | tf_op | source)
XLA Modules:
  0.0 520.4 jit_solution(13407256813020518131)
XLA Ops:
  18.8 5.5 %collective-permute-done.30 = bf16[64,3584]{1,0:T(8,128)(2,1)S(1)} collective-permute-done((bf16[64,3584]{1,0:T(8,128)(2,1)}, bf16[64,3584]{1,0:T(8,128)(2,1)S(1)}, u32[]{:S(2)}, u32[]{:S(2)}) %collective-permute-start.30) | collective-permute-done | bytes 458784 | tf_op jit(solution)/shard_map/ppermute | solution.py:124
  27.9 13.7 %collective-permute-done.1 = bf16[2,64,3584]{2,1,0:T(8,128)(2,1)S(1)} collective-permute-done((bf16[2,64,3584]{2,1,0:T(8,128)(2,1)S(1)}, bf16[2,64,3584]{2,1,0:T(8,128)(2,1)S(1)}, u32[]{:S(2)}, u32[]{:S(2)}) %collective-permute-start.1) | collective-permute-done | bytes 917536 | tf_op jit(solution)/shard_map/ppermute | solution.py:124
  43.8 17.9 %collective-permute-done.31 = bf16[2,64,3584]{2,1,0:T(8,128)(2,1)S(1)} collective-permute-done((bf16[2,64,3584]{2,1,0:T(8,128)(2,1)S(1)}, bf16[2,64,3584]{2,1,0:T(8,128)(2,1)S(1)}, u32[]{:S(2)}, u32[]{:S(2)}) %collective-permute-start.31) | collective-permute-done | bytes 917536 | tf_op jit(solution)/shard_map/ppermute | solution.py:124
  70.9 9.9 %collective-permute-done.16 = bf16[64,3584]{1,0:T(8,128)(2,1)S(1)} collective-permute-done((bf16[64,3584]{1,0:T(8,128)(2,1)S(1)}, bf16[64,3584]{1,0:T(8,128)(2,1)S(1)}, u32[]{:S(2)}, u32[]{:S(2)}) %collective-permute-start.16) | collective-permute-done | bytes 458784 | tf_op jit(solution)/shard_map/ppermute | solution.py:124
  84.6 17.6 %collective-permute-done.17 = bf16[2,64,3584]{2,1,0:T(8,128)(2,1)S(1)} collective-permute-done((bf16[2,64,3584]{2,1,0:T(8,128)(2,1)S(1)}, bf16[2,64,3584]{2,1,0:T(8,128)(2,1)S(1)}, u32[]{:S(2)}, u32[]{:S(2)}) %collective-permute-start.17) | collective-permute-done | bytes 917536 | tf_op jit(solution)/shard_map/ppermute | solution.py:124
  104.9 17.5 %collective-permute-done.45 = bf16[2,64,3584]{2,1,0:T(8,128)(2,1)S(1)} collective-permute-done((bf16[2,64,3584]{2,1,0:T(8,128)(2,1)S(1)}, bf16[2,64,3584]{2,1,0:T(8,128)(2,1)S(1)}, u32[]{:S(2)}, u32[]{:S(2)}) %collective-permute-start.45) | collective-permute-done | bytes 917536 | tf_op jit(solution)/shard_map/ppermute | solution.py:124
  135.1 4.6 collective-permute-done.38
  143.6 4.6 collective-permute-done.20
  150.5 6.1 %collective-permute-done.48 = bf16[64,3584]{1,0:T(8,128)(2,1)S(1)} collective-permute-done((bf16[64,3584]{1,0:T(8,128)(2,1)S(1)}, bf16[64,3584]{1,0:T(8,128)(2,1)S(1)}, u32[]{:S(2)}, u32[]{:S(2)}) %collective-permute-start.48) | collective-permute-done | bytes 458784 | tf_op jit(solution)/shard_map/ppermute | solution.py:124
  159.1 5.4 %collective-permute-start.39 = (bf16[64,3584]{1,0:T(8,128)(2,1)}, bf16[64,3584]{1,0:T(8,128)(2,1)}, u32[]{:S(2)}, u32[]{:S(2)}) collective-permute-start(bf16[64,3584]{1,0:T(8,128)(2,1)} %collective-permute-done.38), channel_id=1, source_target_pairs={{16,24},{18,26},{20,28},{22,30},{17,25},{19,27},{21,29},{23,31}} | collective-permute-start | bytes 1376264 | tf_op jit(solution)/shard_map/ppermute | solution.py:128
  173.6 6.6 %multiply_reduce_fusion.2 = (f32[256]{0:T(256)S(1)}, f32[256,1024]{1,0:T(8,128)}) fusion(f32[256,1024]{1,0:T(8,128)} %fusion.18, bf16[512,3584]{1,0:T(8,128)(2,1)} %copy-done.37, bf16[512,3584]{1,0:T(8,128)(2,1)} %bitcast.293, bf16[64,3584]{1,0:T(8,128)(2,1)} %get-tuple-element.58, bf16[64,3584]{1,0:T(8,128)(2,1)S(1)} %collective-permute-done.44, ...), kind=kOutput, calls=%fused_computation.133 | convolution fusion | flops 1903689472 | bytes 11273216 | tf_op jit(solution)/shard_map/dot_general | solution.py:185
  186.4 11.8 %collective-permute-done.49 = bf16[2,64,3584]{2,1,0:T(8,128)(2,1)S(1)} collective-permute-done((bf16[2,64,3584]{2,1,0:T(8,128)(2,1)}, bf16[2,64,3584]{2,1,0:T(8,128)(2,1)S(1)}, u32[]{:S(2)}, u32[]{:S(2)}) %collective-permute-start.49) | collective-permute-done | bytes 917536 | tf_op jit(solution)/shard_map/ppermute | solution.py:124
  210.3 6.3 %collective-permute-done.40 = bf16[64,3584]{1,0:T(8,128)(2,1)S(1)} collective-permute-done((bf16[64,3584]{1,0:T(8,128)(2,1)S(1)}, bf16[64,3584]{1,0:T(8,128)(2,1)S(1)}, u32[]{:S(2)}, u32[]{:S(2)}) %collective-permute-start.40) | collective-permute-done | bytes 458784 | tf_op jit(solution)/shard_map/ppermute | solution.py:124
  218.8 7.5 %collective-permute-done.13 = bf16[2,64,3584]{2,1,0:T(8,128)(2,1)S(1)} collective-permute-done((bf16[2,64,3584]{2,1,0:T(8,128)(2,1)S(1)}, bf16[2,64,3584]{2,1,0:T(8,128)(2,1)S(1)}, u32[]{:S(2)}, u32[]{:S(2)}) %collective-permute-start.13) | collective-permute-done | bytes 917536 | tf_op jit(solution)/shard_map/ppermute | solution.py:124
  249.3 4.3 collective-permute-start.61
  256.5 33.3 %all-gather = f32[16,64,16]{1,2,0:T(8,128)S(1)} all-gather(f32[1,64,16]{1,2,0:T(8,128)S(1)} %bitcast.280), channel_id=1, replica_groups=mesh['expert'=16,'tok'=2] {'expert'}, dimensions={0}, use_global_device_ids=true | all-gather | bytes 69632 | tf_op jit(solution)/shard_map/all_gather | solution.py:206
  294.7 5.3 %convolution_convert_fusion.5 = bf16[256,3584]{1,0:T(8,128)(2,1)S(1)} fusion(bf16[256,1024]{1,0:T(8,128)(2,1)S(1)} %get-tuple-element.43, bf16[3584,512]{1,0:T(8,128)(2,1)} %copy-done.40, bf16[3584,512]{1,0:T(8,128)(2,1)} %bitcast.284), kind=kOutput, calls=%fused_computation.16 | convolution fusion | flops 1894645760 | bytes 9699328 | tf_op jit(solution)/shard_map/dot_general | solution.py:185
  310.1 5.3 %convolution_convert_fusion.4 = bf16[256,3584]{1,0:T(8,128)(2,1)S(1)} fusion(bf16[256,1024]{1,0:T(8,128)(2,1)S(1)} %get-tuple-element.49, bf16[3584,512]{1,0:T(8,128)(2,1)} %copy-done.40, bf16[3584,512]{1,0:T(8,128)(2,1)} %bitcast.285), kind=kOutput, calls=%fused_computation.15 | convolution fusion | flops 1894645760 | bytes 9699328 | tf_op jit(solution)/shard_map/dot_general | solution.py:185
  315.4 5.3 %convolution_convert_fusion.2 = bf16[256,3584]{1,0:T(8,128)(2,1)S(1)} fusion(bf16[256,1024]{1,0:T(8,128)(2,1)S(1)} %get-tuple-element.47, bf16[3584,512]{1,0:T(8,128)(2,1)} %copy-done.40, bf16[3584,512]{1,0:T(8,128)(2,1)} %bitcast.286), kind=kOutput, calls=%fused_computation.13 | convolution fusion | flops 1894645760 | bytes 9699328 | tf_op jit(solution)/shard_map/dot_general | solution.py:185
  334.3 5.2 %convolution_convert_fusion.8 = bf16[256,3584]{1,0:T(8,128)(2,1)S(1)} fusion(bf16[256,1024]{1,0:T(8,128)(2,1)S(1)} %get-tuple-element.50, bf16[512,3584]{1,0:T(8,128)(2,1)} %copy-done.37, bf16[512,3584]{1,0:T(8,128)(2,1)} %bitcast.294), kind=kOutput, calls=%fused_computation.19 | convolution fusion | flops 1894645760 | bytes 9699328 | tf_op jit(solution)/shard_map/dot_general | solution.py:232
  339.6 5.2 %convolution_convert_fusion.6 = bf16[256,3584]{1,0:T(8,128)(2,1)S(1)} fusion(bf16[256,1024]{1,0:T(8,128)(2,1)S(1)} %get-tuple-element.48, bf16[512,3584]{1,0:T(8,128)(2,1)} %copy-done.37, bf16[512,3584]{1,0:T(8,128)(2,1)} %bitcast.295), kind=kOutput, calls=%fused_computation.17 | convolution fusion | flops 1894645760 | bytes 9699328 | tf_op jit(solution)/shard_map/dot_general | solution.py:232
  345.2 8.6 %convolution_convert_fusion = bf16[512,3584]{1,0:T(8,128)(2,1)} fusion(bf16[1024,3584]{1,0:T(8,128)(2,1)} %constant_dynamic-update-slice_fusion.16, bf16[1024,1024]{1,0:T(8,128)(2,1)S(1)} %pad_maximum_fusion.3), kind=kOutput, calls=%fused_computation.9 | convolution fusion | flops 3759931392 | bytes 12058624 | tf_op jit(solution)/shard_map/dot_general | solution.py:191
  353.8 8.6 %convolution_convert_fusion.1 = bf16[3584,512]{1,0:T(8,128)(2,1)} fusion(bf16[1024,3584]{1,0:T(8,128)(2,1)} %constant_dynamic-update-slice_fusion, bf16[1024,1024]{1,0:T(8,128)(2,1)S(1)} %pad_maximum_fusion.2), kind=kOutput, calls=%fused_computation.10 | convolution fusion | flops 3759931392 | bytes 12058624 | tf_op jit(solution)/shard_map/dot_general | solution.py:191
  367.8 17.8 %collective-permute-done.18 = bf16[2,64,3584]{2,1,0:T(8,128)(2,1)S(1)} collective-permute-done((bf16[2,64,3584]{2,1,0:T(8,128)(2,1)S(1)}, bf16[2,64,3584]{2,1,0:T(8,128)(2,1)S(1)}, u32[]{:S(2)}, u32[]{:S(2)}) %collective-permute-start.18) | collective-permute-done | bytes 917536 | tf_op jit(solution)/shard_map/ppermute | solution.py:124
  385.8 24.3 %collective-permute-done.14 = bf16[2,64,3584]{2,1,0:T(8,128)(2,1)S(1)} collective-permute-done((bf16[2,64,3584]{2,1,0:T(8,128)(2,1)S(1)}, bf16[2,64,3584]{2,1,0:T(8,128)(2,1)S(1)}, u32[]{:S(2)}, u32[]{:S(2)}) %collective-permute-start.14) | collective-permute-done | bytes 917536 | tf_op jit(solution)/shard_map/ppermute | solution.py:124
  413.5 11.1 %collective-permute-done.43 = bf16[64,3584]{1,0:T(8,128)(2,1)S(1)} collective-permute-done((bf16[64,3584]{1,0:T(8,128)(2,1)S(1)}, bf16[64,3584]{1,0:T(8,128)(2,1)S(1)}, u32[]{:S(2)}, u32[]{:S(2)}) %collective-permute-start.43) | collective-permute-done | bytes 458784 | tf_op jit(solution)/shard_map/ppermute | solution.py:124
  428.5 13.1 %collective-permute-done.55 = bf16[64,3584]{1,0:T(8,128)(2,1)S(1)} collective-permute-done((bf16[64,3584]{1,0:T(8,128)(2,1)S(1)}, bf16[64,3584]{1,0:T(8,128)(2,1)S(1)}, u32[]{:S(2)}, u32[]{:S(2)}) %collective-permute-start.55) | collective-permute-done | bytes 458784 | tf_op jit(solution)/shard_map/ppermute | solution.py:128
  444.0 12.2 %collective-permute-done.27 = bf16[64,3584]{1,0:T(8,128)(2,1)S(1)} collective-permute-done((bf16[64,3584]{1,0:T(8,128)(2,1)S(1)}, bf16[64,3584]{1,0:T(8,128)(2,1)S(1)}, u32[]{:S(2)}, u32[]{:S(2)}) %collective-permute-start.27) | collective-permute-done | bytes 458784 | tf_op jit(solution)/shard_map/ppermute | solution.py:128
  457.5 4.6 collective-permute-start.56
  497.6 4.7 collective-permute-done.29
  504.4 7.1 %fusion = bf16[1,3584,512]{2,1,0:T(8,128)(2,1)} fusion(bf16[3584,512]{1,0:T(8,128)(2,1)} %collective-permute-done.62, bf16[1024,3584]{1,0:T(8,128)(2,1)S(1)} %bitcast.283, bf16[1024,1024]{1,0:T(8,128)(2,1)S(1)} %pad_maximum_fusion.2), kind=kOutput, calls=%fused_computation.11 | convolution fusion | flops 3763601408 | bytes 15728640 | tf_op jit(solution)/shard_map/dot_general | solution.py:191
  511.5 8.7 %fusion.1 = bf16[1,512,3584]{2,1,0:T(8,128)(2,1)} fusion(bf16[512,3584]{1,0:T(8,128)(2,1)S(1)} %collective-permute-done.63, bf16[1024,3584]{1,0:T(8,128)(2,1)} %constant_dynamic-update-slice_fusion.16, bf16[1024,1024]{1,0:T(8,128)(2,1)S(1)} %pad_maximum_fusion.3), kind=kOutput, calls=%fused_computation.12 | convolution fusion | flops 3763601408 | bytes 15728640 | tf_op jit(solution)/shard_map/dot_general | solution.py:191
  (324 shorter events, 198.7 us)
Async XLA Ops:
  0.6 62.6 %collective-permute-start.6 = (bf16[64,3584]{1,0:T(8,128)(2,1)}, bf16[64,3584]{1,0:T(8,128)(2,1)S(1)}, u32[]{:S(2)}, u32[]{:S(2)}) collective-permute-start(bf16[64,3584]{1,0:T(8,128)(2,1)} %param.6), channel_id=1, source_target_pairs={{24,16},{26,18},{28,20},{30,22},{16,8},{18,10},{20,12},{22,14},{8,... | collective-permute-start | bytes 1376264 | tf_op jit(solution)/shard_map/ppermute | solution.py:128
  4.7 59.2 %collective-permute-start.9 = (bf16[64,3584]{1,0:T(8,128)(2,1)}, bf16[64,3584]{1,0:T(8,128)(2,1)S(1)}, u32[]{:S(2)}, u32[]{:S(2)}) collective-permute-start(bf16[64,3584]{1,0:T(8,128)(2,1)} %param.6), channel_id=1, source_target_pairs={{0,8},{2,10},{4,12},{6,14},{8,16},{10,18},{12,20},{14,22},{16,24},... | collective-permute-start | bytes 1376264 | tf_op jit(solution)/shard_map/ppermute | solution.py:128
  8.2 60.5 %collective-permute-start.34 = (bf16[64,3584]{1,0:T(8,128)(2,1)}, bf16[64,3584]{1,0:T(8,128)(2,1)S(1)}, u32[]{:S(2)}, u32[]{:S(2)}) collective-permute-start(bf16[64,3584]{1,0:T(8,128)(2,1)} %param.9), channel_id=1, source_target_pairs={{24,16},{26,18},{28,20},{30,22},{16,8},{18,10},{20,12},{22,14},{8,... | collective-permute-start | bytes 1376264 | tf_op jit(solution)/shard_map/ppermute | solution.py:128
  16.5 25.1 %collective-permute-start.1 = (bf16[2,64,3584]{2,1,0:T(8,128)(2,1)S(1)}, bf16[2,64,3584]{2,1,0:T(8,128)(2,1)S(1)}, u32[]{:S(2)}, u32[]{:S(2)}) collective-permute-start(bf16[2,64,3584]{2,1,0:T(8,128)(2,1)S(1)} %pad_maximum_fusion.4), channel_id=1, source_target_pairs={{0,4},{2,6},{4,0},{6,2},{8,12},{10,14},{12,8},{14,10},{16,20},{18,... | collective-permute-start | bytes 2752520 | tf_op jit(solution)/shard_map/ppermute | solution.py:124
  24.3 45.0 %collective-permute-start.37 = (bf16[64,3584]{1,0:T(8,128)(2,1)S(1)}, bf16[64,3584]{1,0:T(8,128)(2,1)S(1)}, u32[]{:S(2)}, u32[]{:S(2)}) collective-permute-start(bf16[64,3584]{1,0:T(8,128)(2,1)S(1)} %copy-done.1), channel_id=1, source_target_pairs={{0,8},{2,10},{4,12},{6,14},{8,16},{10,18},{12,20},{14,22},{16,24},... | collective-permute-start | bytes 1376264 | tf_op jit(solution)/shard_map/ppermute | solution.py:128
  41.6 20.0 %collective-permute-start.31 = (bf16[2,64,3584]{2,1,0:T(8,128)(2,1)S(1)}, bf16[2,64,3584]{2,1,0:T(8,128)(2,1)S(1)}, u32[]{:S(2)}, u32[]{:S(2)}) collective-permute-start(bf16[2,64,3584]{2,1,0:T(8,128)(2,1)S(1)} %pad_maximum_fusion.12), channel_id=1, source_target_pairs={{0,2},{2,0},{4,6},{6,4},{8,10},{10,8},{12,14},{14,12},{16,18},{18,... | collective-permute-start | bytes 2752520 | tf_op jit(solution)/shard_map/ppermute | solution.py:124
  61.7 97.4 %collective-permute-start.2 = (bf16[3584,512]{1,0:T(8,128)(2,1)S(1)}, bf16[3584,512]{1,0:T(8,128)(2,1)S(1)}, u32[]{:S(2)}, u32[]{:S(2)}) collective-permute-start(bf16[3584,512]{1,0:T(8,128)(2,1)S(1)} %bitcast.287), channel_id=1, source_target_pairs={{0,1},{1,0},{2,3},{3,2},{4,5},{5,4},{6,7},{7,6},{8,9},{9,8},{10,11... | collective-permute-start | bytes 11010056 | tf_op jit(solution)/shard_map/ppermute | solution.py:219
  63.3 103.3 %collective-permute-start.3 = (bf16[512,3584]{1,0:T(8,128)(2,1)S(1)}, bf16[512,3584]{1,0:T(8,128)(2,1)S(1)}, u32[]{:S(2)}, u32[]{:S(2)}) collective-permute-start(bf16[512,3584]{1,0:T(8,128)(2,1)S(1)} %bitcast.296), channel_id=1, source_target_pairs={{0,1},{1,0},{2,3},{3,2},{4,5},{5,4},{6,7},{7,6},{8,9},{9,8},{10,11... | collective-permute-start | bytes 11010056 | tf_op jit(solution)/shard_map/ppermute | solution.py:220
  63.9 62.9 %collective-permute-start.7 = (bf16[64,3584]{1,0:T(8,128)(2,1)S(1)}, bf16[64,3584]{1,0:T(8,128)(2,1)}, u32[]{:S(2)}, u32[]{:S(2)}) collective-permute-start(bf16[64,3584]{1,0:T(8,128)(2,1)S(1)} %collective-permute-done.6), channel_id=1, source_target_pairs={{16,8},{18,10},{20,12},{22,14},{8,0},{10,2},{12,4},{14,6},{17,9},{... | collective-permute-start | bytes 1376264 | tf_op jit(solution)/shard_map/ppermute | solution.py:128
  81.0 21.2 %collective-permute-start.17 = (bf16[2,64,3584]{2,1,0:T(8,128)(2,1)S(1)}, bf16[2,64,3584]{2,1,0:T(8,128)(2,1)S(1)}, u32[]{:S(2)}, u32[]{:S(2)}) collective-permute-start(bf16[2,64,3584]{2,1,0:T(8,128)(2,1)S(1)} %pad_maximum_fusion.8), channel_id=1, source_target_pairs={{0,4},{2,6},{4,0},{6,2},{8,12},{10,14},{12,8},{14,10},{16,20},{18,... | collective-permute-start | bytes 2752520 | tf_op jit(solution)/shard_map/ppermute | solution.py:124
  82.4 46.4 %collective-permute-start.10 = (bf16[64,3584]{1,0:T(8,128)(2,1)S(1)}, bf16[64,3584]{1,0:T(8,128)(2,1)}, u32[]{:S(2)}, u32[]{:S(2)}) collective-permute-start(bf16[64,3584]{1,0:T(8,128)(2,1)S(1)} %copy-done.14), channel_id=1, source_target_pairs={{8,16},{10,18},{12,20},{14,22},{16,24},{18,26},{20,28},{22,30},{9,... | collective-permute-start | bytes 1376264 | tf_op jit(solution)/shard_map/ppermute | solution.py:128
  102.2 20.2 %collective-permute-start.45 = (bf16[2,64,3584]{2,1,0:T(8,128)(2,1)S(1)}, bf16[2,64,3584]{2,1,0:T(8,128)(2,1)S(1)}, u32[]{:S(2)}, u32[]{:S(2)}) collective-permute-start(bf16[2,64,3584]{2,1,0:T(8,128)(2,1)S(1)} %pad_maximum_fusion.16), channel_id=1, source_target_pairs={{0,2},{2,0},{4,6},{6,4},{8,10},{10,8},{12,14},{14,12},{16,18},{18,... | collective-permute-start | bytes 2752520 | tf_op jit(solution)/shard_map/ppermute | solution.py:124
  128.7 54.4 %collective-permute-start.8 = (bf16[64,3584]{1,0:T(8,128)(2,1)}, bf16[64,3584]{1,0:T(8,128)(2,1)}, u32[]{:S(2)}, u32[]{:S(2)}) collective-permute-start(bf16[64,3584]{1,0:T(8,128)(2,1)} %collective-permute-done.7), channel_id=1, source_target_pairs={{8,0},{10,2},{12,4},{14,6},{9,1},{11,3},{13,5},{15,7}} | collective-permute-start | bytes 1376264 | tf_op jit(solution)/shard_map/ppermute | solution.py:128
  133.0 50.1 %collective-permute-start.11 = (bf16[64,3584]{1,0:T(8,128)(2,1)}, bf16[64,3584]{1,0:T(8,128)(2,1)}, u32[]{:S(2)}, u32[]{:S(2)}) collective-permute-start(bf16[64,3584]{1,0:T(8,128)(2,1)} %collective-permute-done.10), channel_id=1, source_target_pairs={{16,24},{18,26},{20,28},{22,30},{17,25},{19,27},{21,29},{23,31}} | collective-permute-start | bytes 1376264 | tf_op jit(solution)/shard_map/ppermute | solution.py:128
  156.7 46.2 %collective-permute-start.36 = (bf16[64,3584]{1,0:T(8,128)(2,1)}, bf16[64,3584]{1,0:T(8,128)(2,1)}, u32[]{:S(2)}, u32[]{:S(2)}) collective-permute-start(bf16[64,3584]{1,0:T(8,128)(2,1)} %collective-permute-done.35), channel_id=1, source_target_pairs={{8,0},{10,2},{12,4},{14,6},{9,1},{11,3},{13,5},{15,7}} | collective-permute-start | bytes 1376264 | tf_op jit(solution)/shard_map/ppermute | solution.py:128
  159.1 43.7 %collective-permute-start.39 = (bf16[64,3584]{1,0:T(8,128)(2,1)}, bf16[64,3584]{1,0:T(8,128)(2,1)}, u32[]{:S(2)}, u32[]{:S(2)}) collective-permute-start(bf16[64,3584]{1,0:T(8,128)(2,1)} %collective-permute-done.38), channel_id=1, source_target_pairs={{16,24},{18,26},{20,28},{22,30},{17,25},{19,27},{21,29},{23,31}} | collective-permute-start | bytes 1376264 | tf_op jit(solution)/shard_map/ppermute | solution.py:128
  180.3 17.9 %collective-permute-start.49 = (bf16[2,64,3584]{2,1,0:T(8,128)(2,1)}, bf16[2,64,3584]{2,1,0:T(8,128)(2,1)S(1)}, u32[]{:S(2)}, u32[]{:S(2)}) collective-permute-start(bf16[2,64,3584]{2,1,0:T(8,128)(2,1)} %pad_maximum_fusion.18), channel_id=1, source_target_pairs={{0,2},{2,0},{4,6},{6,4},{8,10},{10,8},{12,14},{14,12},{16,18},{18,... | collective-permute-start | bytes 2752520 | tf_op jit(solution)/shard_map/ppermute | solution.py:124
  185.4 24.2 %collective-permute-start.12 = (bf16[64,3584]{1,0:T(8,128)(2,1)S(1)}, bf16[64,3584]{1,0:T(8,128)(2,1)S(1)}, u32[]{:S(2)}, u32[]{:S(2)}) collective-permute-start(bf16[64,3584]{1,0:T(8,128)(2,1)S(1)} %get-tuple-element.14), channel_id=1, source_target_pairs={{0,2},{2,0},{4,6},{6,4},{8,10},{10,8},{12,14},{14,12},{16,18},{18,... | collective-permute-start | bytes 1376264 | tf_op jit(solution)/shard_map/ppermute | solution.py:124
  209.7 16.7 %collective-permute-start.13 = (bf16[2,64,3584]{2,1,0:T(8,128)(2,1)S(1)}, bf16[2,64,3584]{2,1,0:T(8,128)(2,1)S(1)}, u32[]{:S(2)}, u32[]{:S(2)}) collective-permute-start(bf16[2,64,3584]{2,1,0:T(8,128)(2,1)S(1)} %pad_maximum_fusion.6), channel_id=1, source_target_pairs={{0,4},{2,6},{4,0},{6,2},{8,12},{10,14},{12,8},{14,10},{16,20},{18,... | collective-permute-start | bytes 2752520 | tf_op jit(solution)/shard_map/ppermute | solution.py:124
  300.2 62.1 %collective-permute-start.32 = (bf16[2,64,3584]{2,1,0:T(8,128)(2,1)S(1)}, bf16[2,64,3584]{2,1,0:T(8,128)(2,1)S(1)}, u32[]{:S(2)}, u32[]{:S(2)}) collective-permute-start(bf16[2,64,3584]{2,1,0:T(8,128)(2,1)S(1)} %pad_maximum_fusion.13), channel_id=1, source_target_pairs={{0,2},{2,0},{4,6},{6,4},{8,10},{10,8},{12,14},{14,12},{16,18},{18,... | collective-permute-start | bytes 2752520 | tf_op jit(solution)/shard_map/ppermute | solution.py:124
  307.1 55.4 %collective-permute-start.46 = (bf16[2,64,3584]{2,1,0:T(8,128)(2,1)S(1)}, bf16[2,64,3584]{2,1,0:T(8,128)(2,1)}, u32[]{:S(2)}, u32[]{:S(2)}) collective-permute-start(bf16[2,64,3584]{2,1,0:T(8,128)(2,1)S(1)} %pad_maximum_fusion.17), channel_id=1, source_target_pairs={{0,2},{2,0},{4,6},{6,4},{8,10},{10,8},{12,14},{14,12},{16,18},{18,... | collective-permute-start | bytes 2752520 | tf_op jit(solution)/shard_map/ppermute | solution.py:124
  320.9 44.8 %collective-permute-start.50 = (bf16[2,64,3584]{2,1,0:T(8,128)(2,1)S(1)}, bf16[2,64,3584]{2,1,0:T(8,128)(2,1)S(1)}, u32[]{:S(2)}, u32[]{:S(2)}) collective-permute-start(bf16[2,64,3584]{2,1,0:T(8,128)(2,1)S(1)} %pad_maximum_fusion.19), channel_id=1, source_target_pairs={{0,2},{2,0},{4,6},{6,4},{8,10},{10,8},{12,14},{14,12},{16,18},{18,... | collective-permute-start | bytes 2752520 | tf_op jit(solution)/shard_map/ppermute | solution.py:124
  322.1 43.8 %collective-permute-start.42 = (bf16[2,64,3584]{2,1,0:T(8,128)(2,1)S(1)}, bf16[2,64,3584]{2,1,0:T(8,128)(2,1)S(1)}, u32[]{:S(2)}, u32[]{:S(2)}) collective-permute-start(bf16[2,64,3584]{2,1,0:T(8,128)(2,1)S(1)} %pad_maximum_fusion.15), channel_id=1, source_target_pairs={{0,2},{2,0},{4,6},{6,4},{8,10},{10,8},{12,14},{14,12},{16,18},{18,... | collective-permute-start | bytes 2752520 | tf_op jit(solution)/shard_map/ppermute | solution.py:124
  327.6 38.5 %collective-permute-start.4 = (bf16[2,64,3584]{2,1,0:T(8,128)(2,1)S(1)}, bf16[2,64,3584]{2,1,0:T(8,128)(2,1)}, u32[]{:S(2)}, u32[]{:S(2)}) collective-permute-start(bf16[2,64,3584]{2,1,0:T(8,128)(2,1)S(1)} %pad_maximum_fusion.5), channel_id=1, source_target_pairs={{0,4},{2,6},{4,0},{6,2},{8,12},{10,14},{12,8},{14,10},{16,20},{18,... | collective-permute-start | bytes 2752520 | tf_op jit(solution)/shard_map/ppermute | solution.py:124
  362.3 23.3 %collective-permute-start.18 = (bf16[2,64,3584]{2,1,0:T(8,128)(2,1)S(1)}, bf16[2,64,3584]{2,1,0:T(8,128)(2,1)S(1)}, u32[]{:S(2)}, u32[]{:S(2)}) collective-permute-start(bf16[2,64,3584]{2,1,0:T(8,128)(2,1)S(1)} %pad_maximum_fusion.9), channel_id=1, source_target_pairs={{0,4},{2,6},{4,0},{6,2},{8,12},{10,14},{12,8},{14,10},{16,20},{18,... | collective-permute-start | bytes 2752520 | tf_op jit(solution)/shard_map/ppermute | solution.py:124
  362.5 49.8 %collective-permute-start.22 = (bf16[2,64,3584]{2,1,0:T(8,128)(2,1)S(1)}, bf16[2,64,3584]{2,1,0:T(8,128)(2,1)S(1)}, u32[]{:S(2)}, u32[]{:S(2)}) collective-permute-start(bf16[2,64,3584]{2,1,0:T(8,128)(2,1)S(1)} %pad_maximum_fusion.11), channel_id=1, source_target_pairs={{0,4},{2,6},{4,0},{6,2},{8,12},{10,14},{12,8},{14,10},{16,20},{18,... | collective-permute-start | bytes 2752520 | tf_op jit(solution)/shard_map/ppermute | solution.py:124
  365.7 44.4 %collective-permute-start.14 = (bf16[2,64,3584]{2,1,0:T(8,128)(2,1)S(1)}, bf16[2,64,3584]{2,1,0:T(8,128)(2,1)S(1)}, u32[]{:S(2)}, u32[]{:S(2)}) collective-permute-start(bf16[2,64,3584]{2,1,0:T(8,128)(2,1)S(1)} %pad_maximum_fusion.7), channel_id=1, source_target_pairs={{0,4},{2,6},{4,0},{6,2},{8,12},{10,14},{12,8},{14,10},{16,20},{18,... | collective-permute-start | bytes 2752520 | tf_op jit(solution)/shard_map/ppermute | solution.py:124
  365.9 138.5 %collective-permute-start.62 = (bf16[3584,512]{1,0:T(8,128)(2,1)S(1)}, bf16[3584,512]{1,0:T(8,128)(2,1)}, u32[]{:S(2)}, u32[]{:S(2)}) collective-permute-start(bf16[3584,512]{1,0:T(8,128)(2,1)S(1)} %copy-done.43), channel_id=1, source_target_pairs={{0,1},{1,0},{2,3},{3,2},{4,5},{5,4},{6,7},{7,6},{8,9},{9,8},{10,11... | collective-permute-start | bytes 11010056 | tf_op jit(solution)/shard_map/ppermute | solution.py:250
  366.1 145.4 %collective-permute-start.63 = (bf16[512,3584]{1,0:T(8,128)(2,1)}, bf16[512,3584]{1,0:T(8,128)(2,1)S(1)}, u32[]{:S(2)}, u32[]{:S(2)}) collective-permute-start(bf16[512,3584]{1,0:T(8,128)(2,1)} %convolution_convert_fusion), channel_id=1, source_target_pairs={{0,1},{1,0},{2,3},{3,2},{4,5},{5,4},{6,7},{7,6},{8,9},{9,8},{10,11... | collective-permute-start | bytes 11010056 | tf_op jit(solution)/shard_map/ppermute | solution.py:249
  385.6 41.6 %collective-permute-start.51 = (bf16[64,3584]{1,0:T(8,128)(2,1)S(1)}, bf16[64,3584]{1,0:T(8,128)(2,1)S(1)}, u32[]{:S(2)}, u32[]{:S(2)}) collective-permute-start(bf16[64,3584]{1,0:T(8,128)(2,1)S(1)} %fusion.102), channel_id=1, source_target_pairs={{0,4},{2,6},{4,0},{6,2},{8,12},{10,14},{12,8},{14,10},{16,20},{18,... | collective-permute-start | bytes 1376264 | tf_op jit(solution)/shard_map/ppermute | solution.py:124
  424.8 16.8 %collective-permute-start.55 = (bf16[64,3584]{1,0:T(8,128)(2,1)S(1)}, bf16[64,3584]{1,0:T(8,128)(2,1)S(1)}, u32[]{:S(2)}, u32[]{:S(2)}) collective-permute-start(bf16[64,3584]{1,0:T(8,128)(2,1)S(1)} %add_convert_fusion.7), channel_id=1, source_target_pairs={{24,16},{26,18},{28,20},{30,22},{25,17},{27,19},{29,21},{31,23}} | collective-permute-start | bytes 1376264 | tf_op jit(solution)/shard_map/ppermute | solution.py:128
  443.9 18.4 %collective-permute-start.47 = (bf16[64,3584]{1,0:T(8,128)(2,1)S(1)}, bf16[64,3584]{1,0:T(8,128)(2,1)S(1)}, u32[]{:S(2)}, u32[]{:S(2)}) collective-permute-start(bf16[64,3584]{1,0:T(8,128)(2,1)S(1)} %fusion.104), channel_id=1, source_target_pairs={{0,4},{2,6},{4,0},{6,2},{8,12},{10,14},{12,8},{14,10},{16,20},{18,... | collective-permute-start | bytes 1376264 | tf_op jit(solution)/shard_map/ppermute | solution.py:124
  (78 other events, 1063.1 us)
